TPU v7x, 32 devices: a whole 2x2x4 slice. The times are simulated.
32 devices in a mesh: dp: 4 (over y, x), shard: 8 (over z, core).
Axes of the slice: x: 2, y: 2, z: 4, core: 2. Of those that a mesh axis runs over, the one named last changes fastest.
Arguments:
- layer_input: bfloat16 [384, 46240], P('shard', 'dp'), may hold values from -6 to 6
- cotangent: bfloat16 [32768, 512], P('dp'), may hold values from -0.032958984 to 0.032958984
- momentum: float32 [10368, 512], P('shard'), may hold values from -6 to 6
Outputs:
- momentum_new: float32 [10368, 512], P('shard')
- direction: float32 [10368, 512], P('shard')
All inputs are finite; a program needn't handle non-finite values.
Results may differ from a plain program's by a relative error of at most 0.0003.
Values sent between devices are 32-bit elements; how exact they have to be, the bound alone decides.
No kernel may reach another device: no remote copies, remote signals or barrier semaphores. Data moves between devices by JAX's collectives and lax.ppermute only.
A program may use at most 320 MiB of HBM per device.

v0:
```python
import jax
import jax.numpy as jnp
from jax import lax
from jax.sharding import PartitionSpec as P

HW = 32
ITERS = 2
ROWS = 10368
HIGH = lax.Precision.HIGHEST


def gram_sum(block):
    local = lax.dot_general(block, block, (((0,), (0,)), ((), ())), precision=HIGH)
    return lax.psum(local, "shard")


def body(layer_input, cotangent, momentum):
    chans = layer_input.shape[0]
    voxels = cotangent.shape[0]
    depth = voxels // (HW * HW)
    volume = layer_input.reshape(chans, depth + 2, HW + 2, HW + 2)
    slabs = []
    for kd in range(3):
        for kh in range(3):
            for kw in range(3):
                slabs.append(volume[:, kd : kd + depth, kh : kh + HW, kw : kw + HW])
    patches = jnp.stack(slabs, axis=1).reshape(chans * 27, voxels)
    partial_grad = jnp.dot(patches, cotangent, preferred_element_type=jnp.float32)
    grad = lax.psum(partial_grad, "dp")
    momentum_new = 0.95 * momentum + grad
    squared = lax.psum(jnp.sum(momentum_new * momentum_new), "shard")
    iterate = momentum_new / (jnp.sqrt(squared) + 1e-07)
    gram = gram_sum(iterate)
    for step in range(ITERS):
        if step > 0:
            gram = gram_sum(iterate)
        poly = -4.775 * gram + 2.0315 * jnp.dot(gram, gram, precision=HIGH)
        iterate = 3.4445 * iterate + jnp.dot(iterate, poly, precision=HIGH)
    direction = iterate * jnp.sqrt(jnp.float32(ROWS))
    return (momentum_new, direction)


def solution(mesh):
    return jax.shard_map(
        body,
        mesh=mesh,
        in_specs=(P("shard", "dp"), P("dp", None), P("shard", None)),
        out_specs=(P("shard", None), P("shard", None)),
        check_vma=False,
    )
```

profile of v0, /device:TPU:0, one launch (start us, length us, event | category | flops | bytes accessed | tf_op | source)
XLA Modules:
  0.0 549.4 jit_solution(15928005073139925350)
XLA Ops:
  7.2 0.0 all-reduce.4.cloned.1.call-start
  7.2 8.9 %reshape.10 = bf16[48,10,34,34]{3,2,1,0:T(8,128)(2,1)} reshape(bf16[48,11560]{1,0:T(8,128)(2,1)} %param.3) | data formatting | bytes 2219520 | tf_op jit(solution)/shard_map/reshape | solution.py:21
  16.1 0.0 copy-start
  16.1 4.7 fusion.27
  20.8 0.0 copy-done
  20.8 2.6 fusion.26
  23.4 2.6 fusion.25
  26.0 3.5 fusion.24
  29.5 3.9 fusion.23
  33.4 3.9 fusion.22
  37.3 3.5 fusion.21
  40.8 4.0 fusion.20
  44.9 4.0 fusion.19
  48.9 2.6 fusion.18
  51.5 2.5 fusion.17
  54.1 2.6 fusion.16
  56.7 3.5 fusion.15
  60.2 3.9 fusion.14
  64.1 4.2 fusion.13
  68.2 3.5 fusion.12
  71.7 3.8 fusion.11
  75.6 3.9 fusion.10
  79.4 2.6 fusion.9
  82.0 2.5 fusion.8
  84.5 2.6 fusion.7
  87.1 3.5 fusion.6
  90.6 4.3 fusion.5
  94.9 3.8 fusion.4
  98.8 3.5 fusion.3
  102.3 4.0 fusion.2
  106.3 3.9 fusion.1
  110.2 56.4 %copy.5 = bf16[48,27,8,32,32]{4,3,2,1,0:T(8,128)(2,1)} copy(bf16[48,27,8,32,32]{4,3,2,0,1:T(8,128)(2,1)} %fusion.1) | data formatting | bytes 42467328 | tf_op jit(solution)/shard_map/stack | solution.py:27
  166.5 102.6 %reshape.11 = bf16[1296,8192]{1,0:T(8,128)(2,1)} reshape(bf16[48,27,8,32,32]{4,3,2,1,0:T(8,128)(2,1)} %copy.5) | data formatting | bytes 42467328 | tf_op jit(solution)/shard_map/reshape | solution.py:27
  269.1 0.0 copy-start.1
  269.1 19.1 %fusion.31 = f32[1296,512]{1,0:T(8,128)} fusion(bf16[1296,8192]{1,0:T(8,128)(2,1)} %reshape.11, bf16[8192,512]{1,0:T(8,128)(2,1)} %param.4), kind=kOutput, calls=%fused_computation.65 | convolution fusion | flops 10871635968 | bytes 32276480 | tf_op jit(solution)/shard_map/dot_general | solution.py:28
  288.2 0.0 all-reduce.4.cloned.1.call-update
  288.2 0.0 all-reduce.6.cloned.1.call-start
  288.3 81.9 %all-reduce.4.cloned.1.call-done = f32[1296,512]{1,0:T(8,128)} async-done(((f32[1296,512]{1,0:T(8,128)}), f32[1296,512]{1,0:T(8,128)}) %all-reduce.4.cloned.1.call-update) | async-done | bytes 2654224 | tf_op jit(solution)/shard_map/psum | solution.py:29
  370.2 0.0 copy-done.1
  370.2 4.5 multiply_reduce_fusion
  374.7 17.0 %psum.29 = f32[]{:T(128)} all-reduce(f32[]{:T(128)} %get-tuple-element.2), channel_id=1, replica_groups=mesh['dp'=4,'shard'=8] {'shard'}, use_global_device_ids=true, to_apply=%region_2.0 | all-reduce | flops 1 | bytes 8 | tf_op jit(solution)/shard_map/psum | solution.py:31
  392.4 8.8 %fusion.30 = f32[512,512]{1,0:T(8,128)} fusion(f32[1296,512]{1,0:T(8,128)} %get-tuple-element.3, f32[]{:T(128)S(6)} %add.27), kind=kOutput, calls=%fused_computation.64 | convolution fusion | flops 4077527040 | bytes 3702788 | tf_op jit(solution)/shard_map/dot_general | solution.py:13
  401.1 0.0 all-reduce.6.cloned.1.call-update
  401.1 0.3 all-reduce.8.cloned.1.call-start
  401.4 56.0 %all-reduce.6.cloned.1.call-done = f32[512,512]{1,0:T(8,128)} async-done(((f32[512,512]{1,0:T(8,128)}), f32[512,512]{1,0:T(8,128)}) %all-reduce.6.cloned.1.call-update) | async-done | bytes 1048592 | tf_op jit(solution)/shard_map/psum | solution.py:14
  457.4 3.9 fusion.29
  461.3 6.9 %convolution_add_fusion.1 = f32[1296,512]{1,0:T(8,128)S(1)} fusion(f32[512,512]{1,0:T(8,128)S(1)} %fusion.29, f32[1296,512]{1,0:T(8,128)} %get-tuple-element.3, f32[]{:T(128)S(6)} %add.27), kind=kOutput, calls=%fused_computation.1 | convolution fusion | flops 4079517696 | bytes 6356996 | tf_op jit(solution)/shard_map/dot_general | solution.py:38
  468.2 6.1 %fusion.32 = f32[512,512]{1,0:T(8,128)} fusion(f32[1296,512]{1,0:T(8,128)S(1)} %convolution_add_fusion.1), kind=kOutput, calls=%fused_computation.66 | convolution fusion | flops 4076863488 | bytes 3702784 | tf_op jit(solution)/shard_map/dot_general | solution.py:13
  474.3 0.0 all-reduce.8.cloned.1.call-update
  474.4 57.9 %all-reduce.8.cloned.1.call-done = f32[512,512]{1,0:T(8,128)} async-done(((f32[512,512]{1,0:T(8,128)}), f32[512,512]{1,0:T(8,128)}) %all-reduce.8.cloned.1.call-update) | async-done | bytes 1048592 | tf_op jit(solution)/shard_map/psum | solution.py:14
  532.3 4.2 fusion.28
  536.5 6.1 %fusion = f32[1296,512]{1,0:T(8,128)} fusion(f32[1296,512]{1,0:T(8,128)S(1)} %convolution_add_fusion.1, f32[512,512]{1,0:T(8,128)S(1)} %fusion.28), kind=kOutput, calls=%fused_computation.2 | convolution fusion | flops 4078854144 | bytes 6356992 | tf_op jit(solution)/shard_map/dot_general | solution.py:38
Async XLA Ops:
  7.2 363.1 %all-reduce.4.cloned.1.call-start = ((), (), s32[]{:S(2)}) async-start(), calls=%async_computation | async-start | bytes 5308416 | tf_op jit(solution)/shard_map/psum | solution.py:29
  16.1 4.7 copy-start
  269.1 101.1 %copy-start.1 = (f32[1296,512]{1,0:T(8,128)S(1)}, f32[1296,512]{1,0:T(8,128)}, u32[]{:S(2)}) copy-start(f32[1296,512]{1,0:T(8,128)} %param.5) | copy-start | bytes 7962628
  288.2 169.1 %all-reduce.6.cloned.1.call-start = ((), (), s32[]{:S(2)}) async-start(), calls=%async_computation.1 | async-start | bytes 2097152 | tf_op jit(solution)/shard_map/psum | solution.py:14
  401.1 131.2 %all-reduce.8.cloned.1.call-start = ((), (), s32[]{:S(2)}) async-start(), calls=%async_computation.2 | async-start | bytes 2097152 | tf_op jit(solution)/shard_map/psum | solution.py:14
Sparse Core Ops, SparseCore 0:
  288.4 81.8 all-reduce.3
  401.3 56.0 all-reduce.5
  474.5 57.7 all-reduce.7
where the time goes:
time: 554 us; the launch traced here: 549 us
  local copies, waits for them, and re-layouts  262 us (47%)
  waiting for transfers between devices  196 us (35%)
  matrix products  55.1 us (10%)
  blocking collectives  17 us (3%)
  between operations  14.8 us (3%)
    psum x2, waiting for transfers between devices, gram_sum(): return lax.psum(local, 'shard')  114 us
    reshape x1, local copies, waits for them, and re-layouts, body(): patches = jnp.stack(slabs, axis=1).reshape(chans * 27, voxels)  103 us
    unnamed x30, local copies, waits for them, and re-layouts  90.2 us
    psum x1, waiting for transfers between devices, body(): grad = lax.psum(partial_grad, 'dp')  81.9 us
    another operation x2, local copies, waits for them, and re-layouts, body(): patches = jnp.stack(slabs, axis=1).reshape(chans * 27, voxels)  60.2 us
    dot_general x1, matrix products, body(): jnp.dot(patches, cotangent, preferred_element_type=jnp.float32)  19.1 us
    psum x1, blocking collectives, body(): squared = lax.psum(jnp.sum(momentum_new * momentum_new), 'shard')  17 us
    dot_general x2, matrix products, gram_sum(): lax.dot_general(block, block, (((0,), (0,)), ((), ())), precision=HIGH)  14.9 us
  transfers between devices with their start and end apart: 3, of which 3 were waited for; matrix products, arithmetic and copies ran while one was open for 0% of the time, Pallas kernels for 0%

commit v1 on v0

--- a/solution.py
+++ b/solution.py
@@ -11,7 +11,7 @@
 
 def gram_sum(block):
     local = lax.dot_general(block, block, (((0,), (0,)), ((), ())), precision=HIGH)
-    return lax.psum(local, "shard")
+    return jnp.sum(lax.all_gather(local, "shard"), axis=0)
 
 
 def body(layer_input, cotangent, momentum):

time: 554 us -> 609 us (1.099)
  waiting for transfers between devices: 196 us -> 242 us
  other arithmetic: 4.47 us -> 14.7 us
    all_gather x0 -> x2, waiting for transfers between devices: none -> 160 us  [gram_sum(): return jnp.sum(lax.all_gather(local, 'shard'), axis=0)]
    psum x2 -> x0, waiting for transfers between devices: 114 us -> none  [gram_sum(): return lax.psum(local, 'shard')]
    reduce_sum x0 -> x2, other arithmetic: none -> 10.2 us  [gram_sum(): return jnp.sum(lax.all_gather(local, 'shard'), axis=0)]
where the time goes in v1:
time: 609 us; the launch traced here: 603 us
  local copies, waits for them, and re-layouts  262 us (43%)
  waiting for transfers between devices  242 us (40%)
  matrix products  52.8 us (9%)
  blocking collectives  17 us (3%)
  between operations  14.8 us (2%)
  other arithmetic  14.7 us (2%)
    all_gather x2, waiting for transfers between devices, gram_sum(): return jnp.sum(lax.all_gather(local, 'shard'), axis=0)  160 us
    reshape x1, local copies, waits for them, and re-layouts, body(): patches = jnp.stack(slabs, axis=1).reshape(chans * 27, voxels)  103 us
    unnamed x30, local copies, waits for them, and re-layouts  90.2 us
    psum x1, waiting for transfers between devices, body(): grad = lax.psum(partial_grad, 'dp')  81.9 us
    another operation x2, local copies, waits for them, and re-layouts, body(): patches = jnp.stack(slabs, axis=1).reshape(chans * 27, voxels)  60.2 us
    dot_general x1, matrix products, body(): jnp.dot(patches, cotangent, preferred_element_type=jnp.float32)  19.1 us
    psum x1, blocking collectives, body(): squared = lax.psum(jnp.sum(momentum_new * momentum_new), 'shard')  17 us
    dot_general x2, matrix products, gram_sum(): lax.dot_general(block, block, (((0,), (0,)), ((), ())), precision=HIGH)  14.9 us
  transfers between devices with their start and end apart: 3, of which 3 were waited for; matrix products, arithmetic and copies ran while one was open for 0% of the time, Pallas kernels for 0%

profile of v1, /device:TPU:0, one launch (start us, length us, event | category | flops | bytes accessed | tf_op | source)
XLA Modules:
  0.0 603.3 jit_solution(18246219851619372037)
XLA Ops:
  7.2 0.0 all-reduce.2.cloned.1.call-start
  7.2 8.9 %reshape.10 = bf16[48,10,34,34]{3,2,1,0:T(8,128)(2,1)} reshape(bf16[48,11560]{1,0:T(8,128)(2,1)} %param.3) | data formatting | bytes 2219520 | tf_op jit(solution)/shard_map/reshape | solution.py:21
  16.1 0.0 copy-start
  16.1 4.7 fusion.27
  20.8 0.0 copy-done
  20.8 2.6 fusion.26
  23.4 2.6 fusion.25
  26.0 3.5 fusion.24
  29.5 3.9 fusion.23
  33.4 3.9 fusion.22
  37.3 3.5 fusion.21
  40.8 4.0 fusion.20
  44.9 4.0 fusion.19
  48.9 2.6 fusion.18
  51.5 2.5 fusion.17
  54.1 2.6 fusion.16
  56.7 3.5 fusion.15
  60.2 3.9 fusion.14
  64.1 4.2 fusion.13
  68.2 3.5 fusion.12
  71.7 3.8 fusion.11
  75.6 3.9 fusion.10
  79.4 2.6 fusion.9
  82.0 2.5 fusion.8
  84.5 2.6 fusion.7
  87.1 3.5 fusion.6
  90.6 4.3 fusion.5
  94.9 3.8 fusion.4
  98.8 3.5 fusion.3
  102.3 4.0 fusion.2
  106.3 3.9 fusion.1
  110.2 56.4 %copy.5 = bf16[48,27,8,32,32]{4,3,2,1,0:T(8,128)(2,1)} copy(bf16[48,27,8,32,32]{4,3,2,0,1:T(8,128)(2,1)} %fusion.1) | data formatting | bytes 42467328 | tf_op jit(solution)/shard_map/stack | solution.py:27
  166.5 102.6 %reshape.11 = bf16[1296,8192]{1,0:T(8,128)(2,1)} reshape(bf16[48,27,8,32,32]{4,3,2,1,0:T(8,128)(2,1)} %copy.5) | data formatting | bytes 42467328 | tf_op jit(solution)/shard_map/reshape | solution.py:27
  269.1 0.0 copy-start.1
  269.1 19.1 %fusion.31 = f32[1296,512]{1,0:T(8,128)} fusion(bf16[1296,8192]{1,0:T(8,128)(2,1)} %reshape.11, bf16[8192,512]{1,0:T(8,128)(2,1)} %param.4), kind=kOutput, calls=%fused_computation.65 | convolution fusion | flops 10871635968 | bytes 32276480 | tf_op jit(solution)/shard_map/dot_general | solution.py:28
  288.2 0.0 all-reduce.2.cloned.1.call-update
  288.2 0.0 all-gather.5.cloned.1.call-start
  288.3 81.9 %all-reduce.2.cloned.1.call-done = f32[1296,512]{1,0:T(8,128)} async-done(((f32[1296,512]{1,0:T(8,128)}), f32[1296,512]{1,0:T(8,128)}) %all-reduce.2.cloned.1.call-update) | async-done | bytes 2654224 | tf_op jit(solution)/shard_map/psum | solution.py:29
  370.2 0.0 copy-done.1
  370.2 4.5 multiply_reduce_fusion
  374.7 17.0 %psum.15 = f32[]{:T(128)} all-reduce(f32[]{:T(128)} %get-tuple-element.2), channel_id=1, replica_groups=mesh['dp'=4,'shard'=8] {'shard'}, use_global_device_ids=true, to_apply=%region_2.0 | all-reduce | flops 1 | bytes 8 | tf_op jit(solution)/shard_map/psum | solution.py:31
  392.4 8.8 %fusion.30 = f32[512,512]{1,0:T(8,128)} fusion(f32[1296,512]{1,0:T(8,128)} %get-tuple-element.3, f32[]{:T(128)S(6)} %add.23), kind=kOutput, calls=%fused_computation.64 | convolution fusion | flops 4077527040 | bytes 3702788 | tf_op jit(solution)/shard_map/dot_general | solution.py:13
  401.1 0.0 all-gather.5.cloned.1.call-update
  401.1 0.3 all-gather.7.cloned.1.call-start
  401.4 79.2 %all-gather.5.cloned.1.call-done = f32[4096,512]{1,0:T(8,128)} async-done(((f32[512,512]{1,0:T(8,128)}), f32[4096,512]{1,0:T(8,128)}) %all-gather.5.cloned.1.call-update) | async-done | bytes 8388624 | tf_op jit(solution)/shard_map/all_gather | solution.py:14
  480.6 4.5 reduce_sum.28
  485.1 1.9 fusion.29
  487.0 6.9 %convolution_add_fusion.1 = f32[1296,512]{1,0:T(8,128)S(1)} fusion(f32[512,512]{1,0:T(8,128)S(1)} %fusion.29, f32[1296,512]{1,0:T(8,128)} %get-tuple-element.3, f32[]{:T(128)S(6)} %add.23), kind=kOutput, calls=%fused_computation.1 | convolution fusion | flops 4079517696 | bytes 6356996 | tf_op jit(solution)/shard_map/dot_general | solution.py:38
  493.9 6.1 %fusion.32 = f32[512,512]{1,0:T(8,128)} fusion(f32[1296,512]{1,0:T(8,128)S(1)} %convolution_add_fusion.1), kind=kOutput, calls=%fused_computation.66 | convolution fusion | flops 4076863488 | bytes 3702784 | tf_op jit(solution)/shard_map/dot_general | solution.py:13
  500.0 0.0 all-gather.7.cloned.1.call-update
  500.1 80.7 %all-gather.7.cloned.1.call-done = f32[4096,512]{1,0:T(8,128)} async-done(((f32[512,512]{1,0:T(8,128)}), f32[4096,512]{1,0:T(8,128)}) %all-gather.7.cloned.1.call-update) | async-done | bytes 8388624 | tf_op jit(solution)/shard_map/all_gather | solution.py:14
  580.8 5.7 reduce_sum.29
  586.5 4.0 fusion.28
  590.5 6.1 %fusion = f32[1296,512]{1,0:T(8,128)} fusion(f32[1296,512]{1,0:T(8,128)S(1)} %convolution_add_fusion.1, f32[512,512]{1,0:T(8,128)S(1)} %fusion.28), kind=kOutput, calls=%fused_computation.2 | convolution fusion | flops 4078854144 | bytes 6356992 | tf_op jit(solution)/shard_map/dot_general | solution.py:38
Async XLA Ops:
  7.2 363.1 %all-reduce.2.cloned.1.call-start = ((), (), s32[]{:S(2)}) async-start(), calls=%async_computation | async-start | bytes 5308416 | tf_op jit(solution)/shard_map/psum | solution.py:29
  16.1 4.7 copy-start
  269.1 101.1 %copy-start.1 = (f32[1296,512]{1,0:T(8,128)S(1)}, f32[1296,512]{1,0:T(8,128)}, u32[]{:S(2)}) copy-start(f32[1296,512]{1,0:T(8,128)} %param.5) | copy-start | bytes 7962628
  288.2 192.4 %all-gather.5.cloned.1.call-start = ((), (), s32[]{:S(2)}) async-start(), calls=%async_computation.1 | async-start | bytes 9437184 | tf_op jit(solution)/shard_map/all_gather | solution.py:14
  401.1 179.7 %all-gather.7.cloned.1.call-start = ((), (), s32[]{:S(2)}) async-start(), calls=%async_computation.2 | async-start | bytes 9437184 | tf_op jit(solution)/shard_map/all_gather | solution.py:14
Sparse Core Ops, SparseCore 0:
  288.4 81.8 all-reduce.1
  401.3 79.2 all-gather.4
  500.2 80.5 all-gather.6
